TPU v7x, 32 devices: a whole 2x2x4 slice. The times are simulated.
32 devices in a mesh: band: 4 (over y, x), sector: 8 (over z, core).
Axes of the slice: x: 2, y: 2, z: 4, core: 2. Of those that a mesh axis runs over, the one named last changes fastest.
Arguments:
- grid_lat: bfloat16 [32, 512, 512], P('band', 'sector'), may hold values from -6 to 6
- mesh_lat: bfloat16 [4096, 512], P(('band', 'sector')), may hold values from -6 to 6
- edge_feat: bfloat16 [49152, 512], P(('band', 'sector')), may hold values from -6 to 6
- edge_src: int32 [49152], P(('band', 'sector')), may hold values from 0 to 255, as said below
- edge_dst: int32 [49152], P(('band', 'sector')), may hold values from 0 to 511, as said below
- send_rows: int32 [4096], P(('band', 'sector')), may hold values from 0 to 127
- w_edge1: bfloat16 [1536, 512], replicated, may hold values from -0.15625 to 0.15625
- w_edge2: bfloat16 [512, 512], replicated, may hold values from -0.25 to 0.25
- edge_gain: float32 [512], replicated, may hold values from 0.25 to 1.75
- w_node1: bfloat16 [1024, 512], replicated, may hold values from -0.1875 to 0.1875
- w_node2: bfloat16 [512, 512], replicated, may hold values from -0.25 to 0.25
- node_gain: float32 [512], replicated, may hold values from 0.25 to 1.75
- cotangent: bfloat16 [32, 512, 512], P('band', 'sector'), may hold values from -6 to 6
Outputs:
- grid_out: bfloat16 [32, 512, 512], P('band', 'sector')
- grad_grid: bfloat16 [32, 512, 512], P('band', 'sector')
- grad_mesh: bfloat16 [4096, 512], P(('band', 'sector'))
- grad_w_edge1: float32 [1536, 512], P('sector')
Inputs may be any that keep to these rules, and one draw needn't show every extreme that they name: `edge_src`: A device's mesh table is its 128 own rows followed by 32 rows each from the sector neighbour below, the sector neighbour above, the band neighbour below and the band neighbour above; devices of the first band never read the rows from below, those of the last band never the rows from above. `edge_dst`: each grid point of a device is the destination of exactly 3 of that device's edges; edges are in no particular order.
All inputs are finite; a program needn't handle non-finite values.
Results may differ from a plain program's by a relative error of at most 0.02.
Values may be sent and summed in bfloat16 or wider, within the bound.
A program may use at most 64 MiB of HBM per device.

v0:
```python
import math
import jax
import jax.numpy as jnp
from jax import lax
from jax.sharding import PartitionSpec as P

EPSILON = 1e-05


def with_halo(shard, sides, width, wrap):
    for axis, dim in sides:
        devices, length = (lax.axis_size(axis), shard.shape[dim])
        up = [(i, (i + 1) % devices) for i in range(devices if wrap else devices - 1)]
        down = [(j, i) for i, j in up]
        last = lax.slice_in_dim(shard, length - width, length, axis=dim)
        initial = lax.slice_in_dim(shard, 0, width, axis=dim)
        before = lax.ppermute(last, axis, up)
        after = lax.ppermute(initial, axis, down)
        shard = jnp.concatenate([before, shard, after], axis=dim)
    return shard


def swish(values):
    return values * jax.nn.sigmoid(values)


def layer_norm(values, gain_vector):
    average = jnp.mean(values, axis=-1, keepdims=True)
    centred = values - average
    spread = jnp.mean(centred * centred, axis=-1, keepdims=True)
    return centred * lax.rsqrt(spread + EPSILON) * gain_vector


def decode_tail(pre_act, grid_wide, edge_dst, w_edge2, edge_gain, w_node1, w_node2, node_gain):
    hidden = swish(pre_act).astype(jnp.bfloat16)
    edge_raw = jnp.dot(hidden, w_edge2, preferred_element_type=jnp.float32)
    message = layer_norm(edge_raw, edge_gain).astype(jnp.bfloat16)
    points = grid_wide.shape[0]
    onehot = (edge_dst[None, :] == jnp.arange(points, dtype=jnp.int32)[:, None]).astype(
        jnp.bfloat16
    )
    aggregated = jnp.dot(onehot, message, preferred_element_type=jnp.float32).astype(jnp.bfloat16)
    node_input = jnp.concatenate([aggregated, grid_wide.astype(jnp.bfloat16)], axis=1)
    node_hidden = swish(jnp.dot(node_input, w_node1, preferred_element_type=jnp.float32)).astype(
        jnp.bfloat16
    )
    node_raw = jnp.dot(node_hidden, w_node2, preferred_element_type=jnp.float32)
    return (grid_wide + layer_norm(node_raw, node_gain)).astype(jnp.bfloat16)


def shards(
    grid_lat,
    mesh_lat,
    edge_feat,
    edge_src,
    edge_dst,
    send_rows,
    w_edge1,
    w_edge2,
    edge_gain,
    w_node1,
    w_node2,
    node_gain,
    cotangent,
):
    feature_width = w_edge2.shape[0]
    lat_rows = grid_lat.shape[0]
    lon_cols = grid_lat.shape[1]
    grid_block = grid_lat.reshape(lat_rows * lon_cols, feature_width)
    cot_block = cotangent.reshape(lat_rows * lon_cols, feature_width)
    own_rows = mesh_lat.shape[0]
    margin = send_rows.shape[0] // 4
    picked = jnp.take(mesh_lat, send_rows, axis=0)
    sector_recv = with_halo(picked[: 2 * margin], (("sector", 0),), margin, True)
    band_recv = with_halo(picked[2 * margin :], (("band", 0),), margin, False)
    mesh_table = jnp.concatenate(
        [
            mesh_lat,
            sector_recv[:margin],
            sector_recv[3 * margin :],
            band_recv[:margin],
            band_recv[3 * margin :],
        ],
        axis=0,
    )
    inputs = jnp.concatenate([edge_feat, mesh_table[edge_src], grid_block[edge_dst]], axis=1)
    pre_act = jnp.dot(inputs, w_edge1, preferred_element_type=jnp.float32)
    grid_wide = grid_block.astype(jnp.float32)

    def finish(pre_values, grid_values):
        return decode_tail(
            pre_values, grid_values, edge_dst, w_edge2, edge_gain, w_node1, w_node2, node_gain
        )

    result, pullback = jax.vjp(finish, pre_act, grid_wide)
    grad_pre, grad_tail = pullback(cot_block)
    grad_pre_b = grad_pre.astype(jnp.bfloat16)
    grad_inputs = lax.dot_general(
        grad_pre_b,
        w_edge1[feature_width:],
        (((1,), (1,)), ((), ())),
        preferred_element_type=jnp.float32,
    )
    grad_table = jax.ops.segment_sum(
        grad_inputs[:, :feature_width], edge_src, num_segments=mesh_table.shape[0]
    )
    grad_grid = grad_tail + jax.ops.segment_sum(
        grad_inputs[:, feature_width:], edge_dst, num_segments=grid_block.shape[0]
    )
    sector_back = with_halo(
        grad_table[own_rows : own_rows + 2 * margin].astype(jnp.bfloat16),
        (("sector", 0),),
        margin,
        True,
    ).astype(jnp.float32)
    band_back = with_halo(
        grad_table[own_rows + 2 * margin :].astype(jnp.bfloat16), (("band", 0),), margin, False
    ).astype(jnp.float32)
    returned = jnp.concatenate(
        [
            sector_back[:margin],
            sector_back[3 * margin :],
            band_back[:margin],
            band_back[3 * margin :],
        ],
        axis=0,
    )
    grad_mesh = (
        grad_table[:own_rows] + jax.ops.segment_sum(returned, send_rows, num_segments=own_rows)
    ).astype(jnp.bfloat16)
    total_edges = edge_feat.shape[0] * lax.axis_size("band") * lax.axis_size("sector")
    grad_scale = 1.0 / math.sqrt(total_edges)
    sector_part = lax.psum_scatter(
        lax.dot_general(
            inputs, grad_pre_b, (((0,), (0,)), ((), ())), preferred_element_type=jnp.float32
        ).astype(jnp.bfloat16),
        "sector",
        scatter_dimension=0,
        tiled=True,
    )
    share_rows = lax.psum(sector_part, "band").astype(jnp.float32)
    grad_w_edge1 = share_rows * grad_scale
    grid_out = result.reshape(lat_rows, lon_cols, feature_width)
    grad_grid_out = grad_grid.astype(jnp.bfloat16).reshape(lat_rows, lon_cols, feature_width)
    return (grid_out, grad_grid_out, grad_mesh, grad_w_edge1)


def solution(mesh):
    in_specs = (
        P("band", "sector", None),
        P(("band", "sector"), None),
        P(("band", "sector"), None),
        P(("band", "sector")),
        P(("band", "sector")),
        P(("band", "sector")),
        P(),
        P(),
        P(),
        P(),
        P(),
        P(),
        P("band", "sector", None),
    )
    out_specs = (
        P("band", "sector", None),
        P("band", "sector", None),
        P(("band", "sector"), None),
        P("sector", None),
    )
    return jax.shard_map(shards, mesh=mesh, in_specs=in_specs, out_specs=out_specs, check_vma=False)
```

profile of v0, /device:TPU:0, one launch (start us, length us, event | category | flops | bytes accessed | tf_op | source)
XLA Modules:
  0.0 159.2 jit_solution(11389695265624207588)
XLA Ops:
  7.2 0.8 compare_and_fusion
  8.0 0.7 compare_select_fusion.2
  8.7 1.8 %gather_fusion = bf16[128,512]{1,0:T(8,128)(2,1)S(1)} fusion(bf16[128,512]{1,0:T(8,128)(2,1)} %param.14, s32[1024]{0:T(1024)S(1)} %pad_clamp_fusion.2), kind=kCustom, calls=%fused_computation | custom fusion | bytes 262656 | tf_op jit(solution)/shard_map/jit(_take)/gather | solution.py:73
  10.6 0.7 fusion.66
  11.2 1.3 collective-permute-start.3
  12.5 5.5 %collective-permute-start.2 = (bf16[32,512]{1,0:T(8,128)(2,1)}, bf16[32,512]{1,0:T(8,128)(2,1)S(1)}, u32[]{:S(2)}, u32[]{:S(2)}) collective-permute-start(bf16[32,512]{1,0:T(8,128)(2,1)} %get-tuple-element.20), channel_id=1, source_target_pairs={{0,8},{8,16},{16,24},{1,9},{9,17},{17,25},{2,10},{10,18},{18,26},{... | collective-permute-start | bytes 98312 | tf_op jit(solution)/shard_map/ppermute | solution.py:17
  18.0 3.1 %collective-permute-start.1 = (bf16[32,512]{1,0:T(8,128)(2,1)}, bf16[32,512]{1,0:T(8,128)(2,1)S(1)}, u32[]{:S(2)}, u32[]{:S(2)}) collective-permute-start(bf16[32,512]{1,0:T(8,128)(2,1)} %get-tuple-element.21), channel_id=1, source_target_pairs={{1,0},{2,1},{3,2},{4,3},{5,4},{6,5},{7,6},{0,7},{9,8},{10,9},{11,1... | collective-permute-start | bytes 98312 | tf_op jit(solution)/shard_map/ppermute | solution.py:18
  21.1 0.9 constant_dynamic-update-slice_fusion.4
  22.0 0.7 compare_select_fusion.1
  22.7 0.7 compare_select_fusion
  23.4 2.7 %constant_dynamic-update-slice_fusion.7 = bf16[1536,1536]{1,0:T(8,128)(2,1)} fusion(bf16[1536,512]{1,0:T(8,128)(2,1)} %param.15), kind=kLoop, calls=%fused_computation.96 | loop fusion | bytes 3145728
  26.1 4.8 %gather_fusion.2 = bf16[1536,512]{1,0:T(8,128)(2,1)S(1)} fusion(bf16[512,512]{1,0:T(8,128)(2,1)S(1)} %bitcast.21, s32[2048]{0:T(1024)S(1)} %pad_clamp_fusion), kind=kCustom, calls=%fused_computation.2 | custom fusion | bytes 3151872 | tf_op jit(solution)/shard_map/gather | solution.py:86
  31.0 5.4 %gather_fusion.1 = bf16[1536,512]{1,0:T(8,128)(2,1)} fusion(bf16[256,512]{1,0:T(8,128)(2,1)S(1)} %constant_dynamic-update-slice_fusion, s32[2048]{0:T(1024)S(1)} %pad_clamp_fusion.1), kind=kCustom, calls=%fused_computation.1 | custom fusion | bytes 3151872 | tf_op jit(solution)/shard_map/gather | solution.py:86
  36.5 2.8 %constant_dynamic-update-slice_fusion.6 = bf16[1536,1536]{1,0:T(8,128)(2,1)} fusion(bf16[1536,1536]{1,0:T(8,128)(2,1)} %constant_dynamic-update-slice_fusion.7, bf16[1536,512]{1,0:T(8,128)(2,1)} %gather_fusion.1), kind=kLoop, calls=%fused_computation.95 | loop fusion | bytes 3145728
  39.3 1.3 constant_dynamic-update-slice_fusion.5
  40.6 4.5 %fusion.69 = f32[1536,512]{1,0:T(8,128)S(1)} fusion(bf16[1536,1536]{1,0:T(8,128)(2,1)} %constant_dynamic-update-slice_fusion.5, bf16[1536,512]{1,0:T(8,128)(2,1)S(1)} %copy-done.8), kind=kOutput, calls=%fused_computation.122 | convolution fusion | flops 2415919104 | bytes 9437184 | tf_op jit(solution)/shard_map/dot_general | solution.py:87
  45.1 1.2 fusion.67
  46.3 0.5 copy-done.14
  46.8 0.4 multiply_reduce_fusion.1
  47.2 0.3 copy-done.6
  47.5 1.2 fusion.24
  48.7 0.7 fusion.32
  49.4 0.3 copy-done.9
  49.7 0.5 fusion.68
  50.3 0.5 copy-done.13
  50.7 0.4 copy-done.4
  51.1 0.4 fusion.27
  51.6 1.3 fusion.63
  52.9 3.6 %convolution_convert_fusion.1 = bf16[512,1024]{1,0:T(8,128)(2,1)} fusion(bf16[1024,512]{1,0:T(8,128)(2,1)S(1)} %copy-done, f32[512,512]{1,0:T(8,128)} %copy-done.13, bf16[512,512]{1,0:T(8,128)(2,1)} %param.23, f32[512,512]{1,0:T(8,128)S(1)} %get-tuple-element.7, f32[512]{0:T(512)S(1)} %negate_multiply_fusion.1), kind=kOutput, calls=%fused_computation.40 | convolution fusion | flops 808976384 | bytes 4720640 | tf_op jit(solution)/shard_map/transpose(jvp())/dot_general | solution.py:44
  56.5 3.5 %multiply_reduce_fusion = (f32[1536]{0:T(1024)S(1)}, bf16[1536,512]{0,1:T(8,128)(2,1)S(1)}) fusion(f32[1536,512]{0,1:T(8,128)} %copy-done.2, f32[512]{0:T(512)S(1)} %copy-done.7, f32[1536]{0:T(1024)S(1)} %broadcast_multiply_fusion, bf16[512,1024]{1,0:T(8,128)(2,1)} %convolution_convert_fusion.1, s32[1536]{0:T(1024)S(1)} %copy-done.6), kind=kOutput, calls=%fused_computation.19 | convolution fusion | flops 810809856 | bytes 5263360 | tf_op jit(solution)/shard_map/transpose(jvp())/dot_general | solution.py:42
  60.0 0.9 fusion.45
  61.0 1.0 copy-done.15
  62.0 2.4 %fusion.1 = bf16[1536,512]{1,0:T(8,128)(2,1)S(1)} fusion(f32[1536,512]{1,0:T(8,128)S(1)} %copy-done.15, bf16[512,512]{1,0:T(8,128)(2,1)S(1)} %copy-done.11, f32[1536]{0:T(1024)S(1)} %negate_multiply_fusion, bf16[1536,512]{0,1:T(8,128)(2,1)S(1)} %get-tuple-element.30, f32[1536,512]{0,1:T(8,128)S(1)} %copy-done.3, f32[1536]{0:T(1024)S(1)} %multiply_multiply_fusion, ...), kind=kOutput, calls=%fused_computation.11 | convolution fusion | flops 821035008 | bytes 9988096 | tf_op jit(solution)/shard_map/transpose(jvp())/dot_general | solution.py:36
  64.5 1.2 copy-done.12
  65.7 3.8 %convolution_convert_fusion = bf16[1536,512]{1,0:T(8,128)(2,1)} fusion(bf16[1536,1536]{1,0:T(8,128)(2,1)S(1)} %bitcast.26, bf16[1536,512]{1,0:T(8,128)(2,1)S(1)} %fusion.1), kind=kOutput, calls=%fused_computation.30 | convolution fusion | flops 2416705536 | bytes 7864320 | tf_op jit(solution)/shard_map/dot_general | solution.py:134
  69.5 6.2 %fusion.36 = f32[1536,1024]{1,0:T(8,128)} fusion(bf16[1536,512]{1,0:T(8,128)(2,1)} %copy-done.12, bf16[1536,512]{1,0:T(8,128)(2,1)} %param.19), kind=kOutput, calls=%fused_computation.56 | convolution fusion | flops 1610612736 | bytes 8912896 | tf_op jit(solution)/shard_map/dot_general | solution.py:98
  75.7 10.7 %scatter_custom_fusion.1 = f32[256,512]{1,0:T(8,128)S(1)} fusion(s32[1536]{0:T(1024)} %param.16, f32[1536,1024]{1,0:T(8,128)} %fusion.36, f32[]{:T(128)} %constant.21.clone.1), kind=kCustom, calls=%fused_computation.13 | custom fusion | flops 786432 | bytes 3670528 | tf_op jit(solution)/shard_map/scatter-add | solution.py:104
  86.5 1.3 collective-permute-start.7
  87.8 4.9 %collective-permute-start.6 = (bf16[32,512]{1,0:T(8,128)(2,1)S(1)}, bf16[32,512]{1,0:T(8,128)(2,1)S(1)}, u32[]{:S(2)}, u32[]{:S(2)}) collective-permute-start(bf16[32,512]{1,0:T(8,128)(2,1)S(1)} %get-tuple-element.11), channel_id=1, source_target_pairs={{0,8},{8,16},{16,24},{1,9},{9,17},{17,25},{2,10},{10,18},{18,26},{... | collective-permute-start | bytes 98312 | tf_op jit(solution)/shard_map/ppermute | solution.py:17
  92.6 1.2 convert_add_fusion
  93.9 10.9 %scatter_custom_fusion = f32[512,512]{1,0:T(8,128)S(1)} fusion(f32[512,512]{1,0:T(8,128)S(1)} %convert_add_fusion, s32[1536]{0:T(1024)S(1)} %copy-done.6, f32[1536,1024]{1,0:T(8,128)} %fusion.36), kind=kCustom, calls=%fused_computation.15 | custom fusion | flops 786432 | bytes 4194304 | tf_op jit(solution)/shard_map/scatter-add | solution.py:107
  104.7 0.9 convert_element_type.91
  105.6 3.5 %collective-permute-start.5 = (bf16[32,512]{1,0:T(8,128)(2,1)S(1)}, bf16[32,512]{1,0:T(8,128)(2,1)S(1)}, u32[]{:S(2)}, u32[]{:S(2)}) collective-permute-start(bf16[32,512]{1,0:T(8,128)(2,1)S(1)} %get-tuple-element.12), channel_id=1, source_target_pairs={{1,0},{2,1},{3,2},{4,3},{5,4},{6,5},{7,6},{0,7},{9,8},{10,9},{11,1... | collective-permute-start | bytes 98312 | tf_op jit(solution)/shard_map/ppermute | solution.py:18
  109.2 1.5 collective-permute-done.4
  110.8 1.6 %scatter_custom_fusion.2 = f32[128,512]{1,0:T(8,128)S(1)} fusion(f32[128,512]{1,0:T(8,128)S(1)} %slice.96, s32[128]{0:T(128)} %param.18, f32[32,512]{1,0:T(8,128)S(1)} %get-tuple-element.18, f32[]{:T(128)} %constant.48, f32[32,512]{1,0:T(8,128)S(1)} %get-tuple-element.17, f32[32,512]{1,0:T(8,128)S(1)} %get-tuple-element.16, f32[32,512]{1,0:T(8,128)S(1)} %get-tuple-element.15), kind=kCustom, calls=%fused_computation.69 | custom fusion | flops 262144 | bytes 524800 | tf_op jit(solution)/shard_map/scatter-add | solution.py:129
  112.4 0.7 convert_element_type.94
  113.1 37.6 %all-reduce.2.cloned.1.call-done = bf16[192,512]{1,0:T(8,128)(2,1)} async-done(((bf16[192,512]{1,0:T(8,128)(2,1)}), bf16[192,512]{1,0:T(8,128)(2,1)}) %all-reduce.2.cloned.1.call-update) | async-done | bytes 196624 | tf_op jit(solution)/shard_map/psum | solution.py:141
  150.6 1.7 %convert_multiply_fusion.6 = f32[192,512]{1,0:T(8,128)} fusion(bf16[192,512]{1,0:T(8,128)(2,1)} %all-reduce.2.cloned.1.call-done), kind=kLoop, calls=%fused_computation.68 | loop fusion | flops 196608 | bytes 589824 | tf_op jit(solution)/shard_map/mul | solution.py:142
  (65 shorter events, 0.6 us)
Async XLA Ops:
  7.2 41.5 %copy-start = (bf16[1024,512]{1,0:T(8,128)(2,1)S(1)}, bf16[1024,512]{1,0:T(8,128)(2,1)}, u32[]{:S(2)}) copy-start(bf16[1024,512]{1,0:T(8,128)(2,1)} %param.22) | copy-start | bytes 3145732
  7.2 19.0 %copy-start.1 = (bf16[8,64,512]{2,1,0:T(8,128)(2,1)S(1)}, bf16[8,64,512]{2,1,0:T(8,128)(2,1)}, u32[]{:S(2)}) copy-start(bf16[8,64,512]{2,1,0:T(8,128)(2,1)} %param.13) | copy-start | bytes 1572868
  7.2 102.0 %reduce-scatter.2.cloned.1.call-start = ((), (), s32[]{:S(2)}) async-start(), calls=%async_computation.1 | async-start | bytes 1769472 | tf_op jit(solution)/shard_map/reduce_scatter | solution.py:133
  11.2 19.8 %collective-permute-start.3 = (bf16[32,512]{1,0:T(8,128)(2,1)}, bf16[32,512]{1,0:T(8,128)(2,1)S(1)}, u32[]{:S(2)}, u32[]{:S(2)}) collective-permute-start(bf16[32,512]{1,0:T(8,128)(2,1)} %get-tuple-element.19), channel_id=1, source_target_pairs={{8,0},{16,8},{24,16},{9,1},{17,9},{25,17},{10,2},{18,10},{26,18},{... | collective-permute-start | bytes 98312 | tf_op jit(solution)/shard_map/ppermute | solution.py:18
  12.5 18.5 %collective-permute-start.2 = (bf16[32,512]{1,0:T(8,128)(2,1)}, bf16[32,512]{1,0:T(8,128)(2,1)S(1)}, u32[]{:S(2)}, u32[]{:S(2)}) collective-permute-start(bf16[32,512]{1,0:T(8,128)(2,1)} %get-tuple-element.20), channel_id=1, source_target_pairs={{0,8},{8,16},{16,24},{1,9},{9,17},{17,25},{2,10},{10,18},{18,26},{... | collective-permute-start | bytes 98312 | tf_op jit(solution)/shard_map/ppermute | solution.py:17
  18.0 13.0 %collective-permute-start.1 = (bf16[32,512]{1,0:T(8,128)(2,1)}, bf16[32,512]{1,0:T(8,128)(2,1)S(1)}, u32[]{:S(2)}, u32[]{:S(2)}) collective-permute-start(bf16[32,512]{1,0:T(8,128)(2,1)} %get-tuple-element.21), channel_id=1, source_target_pairs={{1,0},{2,1},{3,2},{4,3},{5,4},{6,5},{7,6},{0,7},{9,8},{10,9},{11,1... | collective-permute-start | bytes 98312 | tf_op jit(solution)/shard_map/ppermute | solution.py:18
  21.1 9.9 %collective-permute-start = (bf16[32,512]{1,0:T(8,128)(2,1)}, bf16[32,512]{1,0:T(8,128)(2,1)S(1)}, u32[]{:S(2)}, u32[]{:S(2)}) collective-permute-start(bf16[32,512]{1,0:T(8,128)(2,1)} %get-tuple-element.22), channel_id=1, source_target_pairs={{0,1},{1,2},{2,3},{3,4},{4,5},{5,6},{6,7},{7,0},{8,9},{9,10},{10,1... | collective-permute-start | bytes 98312 | tf_op jit(solution)/shard_map/ppermute | solution.py:17
  36.5 4.1 %copy-start.8 = (bf16[1536,512]{1,0:T(8,128)(2,1)S(1)}, bf16[1536,512]{1,0:T(8,128)(2,1)}, u32[]{:S(2)}) copy-start(bf16[1536,512]{1,0:T(8,128)(2,1)} %param.19) | copy-start | bytes 4718596
  40.6 4.5 %copy-start.10 = (bf16[512,512]{1,0:T(8,128)(2,1)S(1)}, bf16[512,512]{1,0:T(8,128)(2,1)}, u32[]{:S(2)}) copy-start(bf16[512,512]{1,0:T(8,128)(2,1)} %param.20) | copy-start | bytes 1572868
  45.1 1.6 %copy-start.14 = (f32[1536,512]{1,0:T(8,128)}, f32[1536,512]{1,0:T(8,128)S(1)}, u32[]{:S(2)}) copy-start(f32[1536,512]{1,0:T(8,128)S(1)} %fusion.69) | copy-start | bytes 9437188
  46.8 1.9 %copy-start.2 = (f32[1536,512]{0,1:T(8,128)}, f32[1536,512]{0,1:T(8,128)S(1)}, u32[]{:S(2)}) copy-start(f32[1536,512]{0,1:T(8,128)S(1)} %get-tuple-element.26) | copy-start | bytes 9437188
  46.8 0.7 copy-start.6
  46.8 0.7 copy-start.7
  48.7 1.0 copy-start.9
  49.7 1.0 copy-start.13
  49.7 1.4 copy-start.4
  49.7 1.4 copy-start.5
  56.5 3.5 %copy-start.3 = (f32[1536,512]{0,1:T(8,128)S(1)}, f32[1536,512]{0,1:T(8,128)}, u32[]{:S(2)}) copy-start(f32[1536,512]{0,1:T(8,128)} %copy-done.2) | copy-start | bytes 9437188
  60.0 1.0 copy-start.11
  60.0 2.1 %copy-start.15 = (f32[1536,512]{1,0:T(8,128)S(1)}, f32[1536,512]{1,0:T(8,128)}, u32[]{:S(2)}) copy-start(f32[1536,512]{1,0:T(8,128)} %copy-done.14) | copy-start | bytes 9437188
  60.0 5.7 %slice-start = ((s8[4718592]{0:T(1024)(128)(4,1)}), s8[4194304]{0:T(1024)(128)(4,1)S(1)}, s32[]{:S(2)}) async-start(s8[4718592]{0:T(1024)(128)(4,1)} %bitcast.25), calls=%async_computation.3 | async-start | bytes 8388608
  62.0 3.7 %slice-start.1 = ((s8[4718592]{0:T(1024)(128)(4,1)}), s8[524288]{0:T(1024)(128)(4,1)S(1)}, s32[]{:S(2)}) async-start(s8[4718592]{0:T(1024)(128)(4,1)} %bitcast.25), calls=%async_computation.4 | async-start | bytes 1048576
  64.5 1.2 copy-start.12
  69.5 81.1 %all-reduce.2.cloned.1.call-start = ((), (), s32[]{:S(2)}) async-start(), calls=%async_computation.2 | async-start | bytes 393216 | tf_op jit(solution)/shard_map/psum | solution.py:141
  86.5 22.7 %collective-permute-start.7 = (bf16[32,512]{1,0:T(8,128)(2,1)S(1)}, bf16[32,512]{1,0:T(8,128)(2,1)S(1)}, u32[]{:S(2)}, u32[]{:S(2)}) collective-permute-start(bf16[32,512]{1,0:T(8,128)(2,1)S(1)} %get-tuple-element.10), channel_id=1, source_target_pairs={{8,0},{16,8},{24,16},{9,1},{17,9},{25,17},{10,2},{18,10},{26,18},{... | collective-permute-start | bytes 98312 | tf_op jit(solution)/shard_map/ppermute | solution.py:18
  87.8 21.4 %collective-permute-start.6 = (bf16[32,512]{1,0:T(8,128)(2,1)S(1)}, bf16[32,512]{1,0:T(8,128)(2,1)S(1)}, u32[]{:S(2)}, u32[]{:S(2)}) collective-permute-start(bf16[32,512]{1,0:T(8,128)(2,1)S(1)} %get-tuple-element.11), channel_id=1, source_target_pairs={{0,8},{8,16},{16,24},{1,9},{9,17},{17,25},{2,10},{10,18},{18,26},{... | collective-permute-start | bytes 98312 | tf_op jit(solution)/shard_map/ppermute | solution.py:17
  105.6 5.1 %collective-permute-start.4 = (bf16[32,512]{1,0:T(8,128)(2,1)S(1)}, bf16[32,512]{1,0:T(8,128)(2,1)S(1)}, u32[]{:S(2)}, u32[]{:S(2)}) collective-permute-start(bf16[32,512]{1,0:T(8,128)(2,1)S(1)} %get-tuple-element.9), channel_id=1, source_target_pairs={{0,1},{1,2},{2,3},{3,4},{4,5},{5,6},{6,7},{7,0},{8,9},{9,10},{10,1... | collective-permute-start | bytes 98312 | tf_op jit(solution)/shard_map/ppermute | solution.py:17
  105.6 5.1 %collective-permute-start.5 = (bf16[32,512]{1,0:T(8,128)(2,1)S(1)}, bf16[32,512]{1,0:T(8,128)(2,1)S(1)}, u32[]{:S(2)}, u32[]{:S(2)}) collective-permute-start(bf16[32,512]{1,0:T(8,128)(2,1)S(1)} %get-tuple-element.12), channel_id=1, source_target_pairs={{1,0},{2,1},{3,2},{4,3},{5,4},{6,5},{7,6},{0,7},{9,8},{10,9},{11,1... | collective-permute-start | bytes 98312 | tf_op jit(solution)/shard_map/ppermute | solution.py:18
Sparse Core Ops, SparseCore 0:
  69.6 35.2 reduce-scatter.1
  109.3 41.2 all-reduce.1
where the time goes:
time: 160 us; the launch traced here: 159 us
  waiting for transfers between devices  39.1 us (24%)
  other arithmetic  33.7 us (21%)
  matrix products  27.5 us (17%)
  local copies, waits for them, and re-layouts  24.8 us (16%)
  starting transfers between devices  19.6 us (12%)
  between operations  14.4 us (9%)
    psum x1, waiting for transfers between devices, shards(): share_rows = lax.psum(sector_part, 'band').astype(jnp.float32)  37.6 us
    scatter-add x1, other arithmetic, shards(): jax.ops.segment_sum(grad_inputs[:, feature_width:], edge_dst, num_segment...  10.9 us
    unnamed x42, local copies, waits for them, and re-layouts  10.8 us
    scatter-add x1, other arithmetic, shards(): jax.ops.segment_sum(grad_inputs[:, :feature_width], edge_src, num_segment...  10.7 us
    ppermute x4, starting transfers between devices, with_halo(): before = lax.ppermute(last, axis, up)  10.4 us
    ppermute x4, starting transfers between devices, with_halo(): after = lax.ppermute(initial, axis, down)  9.17 us
    dot_general x1, matrix products, shards(): lax.dot_general(grad_pre_b, w_edge1[feature_width:], (((1,), (1,)), ((),...  6.19 us
    gather x1, local copies, waits for them, and re-layouts, shards(): mesh_table[edge_src]  5.42 us
  transfers between devices with their start and end apart: 10, of which 2 were waited for; matrix products, arithmetic and copies ran while one was open for 26% of the time, Pallas kernels for 0%

commit v1 on v0

--- a/solution.py
+++ b/solution.py
@@ -138,7 +138,7 @@
         scatter_dimension=0,
         tiled=True,
     )
-    share_rows = lax.psum(sector_part, "band").astype(jnp.float32)
+    share_rows = lax.all_gather(sector_part, "band").sum(axis=0).astype(jnp.float32)
     grad_w_edge1 = share_rows * grad_scale
     grid_out = result.reshape(lat_rows, lon_cols, feature_width)
     grad_grid_out = grad_grid.astype(jnp.bfloat16).reshape(lat_rows, lon_cols, feature_width)

time: 160 us -> 135 us (0.84)
  waiting for transfers between devices: 39.1 us -> 1.61 us
  blocking collectives: 0 us -> 13.8 us
    psum x1 -> x0, waiting for transfers between devices: 37.6 us -> none  [shards(): share_rows = lax.psum(sector_part, 'band').astype(jnp.float32)]
    all_gather x0 -> x1, blocking collectives: none -> 13.8 us  [shards(): lax.all_gather(sector_part, 'band').sum(axis=0).astype(jnp.float32)]
  transfers between devices with their start and end apart: 10 -> 9, of which waited for: 2 -> 1; matrix products, arithmetic and copies ran while one was open for 26% -> 31% of each run, Pallas kernels for 0% -> 0%
where the time goes in v1:
time: 135 us
  other arithmetic  32.9 us (24%)
  matrix products  27.4 us (20%)
  local copies, waits for them, and re-layouts  24.8 us (18%)
  starting transfers between devices  19.6 us (15%)
  between operations  14.4 us (11%)
  blocking collectives  13.8 us (10%)
  waiting for transfers between devices  1.61 us (1%)
    all_gather x1, blocking collectives, shards(): lax.all_gather(sector_part, 'band').sum(axis=0).astype(jnp.float32)  13.8 us
    scatter-add x1, other arithmetic, shards(): jax.ops.segment_sum(grad_inputs[:, feature_width:], edge_dst, num_segment...  10.9 us
    unnamed x42, local copies, waits for them, and re-layouts  10.8 us
    scatter-add x1, other arithmetic, shards(): jax.ops.segment_sum(grad_inputs[:, :feature_width], edge_src, num_segment...  10.6 us
    ppermute x4, starting transfers between devices, with_halo(): before = lax.ppermute(last, axis, up)  10.4 us
    ppermute x4, starting transfers between devices, with_halo(): after = lax.ppermute(initial, axis, down)  9.17 us
    dot_general x1, matrix products, shards(): lax.dot_general(grad_pre_b, w_edge1[feature_width:], (((1,), (1,)), ((),...  6.17 us
    gather x1, local copies, waits for them, and re-layouts, shards(): mesh_table[edge_src]  5.42 us
  transfers between devices with their start and end apart: 9, of which 1 were waited for; matrix products, arithmetic and copies ran while one was open for 31% of the time, Pallas kernels for 0%

profile of v1, /device:TPU:0, one launch (start us, length us, event | category | flops | bytes accessed | tf_op | source)
XLA Modules:
  0.0 134.5 jit_solution(8833025060417392669)
XLA Ops:
  7.2 0.8 compare_and_fusion
  8.0 0.7 compare_select_fusion.2
  8.7 1.8 %gather_fusion = bf16[128,512]{1,0:T(8,128)(2,1)S(1)} fusion(bf16[128,512]{1,0:T(8,128)(2,1)} %param.14, s32[1024]{0:T(1024)S(1)} %pad_clamp_fusion.2), kind=kCustom, calls=%fused_computation | custom fusion | bytes 262656 | tf_op jit(solution)/shard_map/jit(_take)/gather | solution.py:73
  10.6 0.7 fusion.66
  11.2 1.3 collective-permute-start.3
  12.5 5.5 %collective-permute-start.2 = (bf16[32,512]{1,0:T(8,128)(2,1)}, bf16[32,512]{1,0:T(8,128)(2,1)S(1)}, u32[]{:S(2)}, u32[]{:S(2)}) collective-permute-start(bf16[32,512]{1,0:T(8,128)(2,1)} %get-tuple-element.20), channel_id=1, source_target_pairs={{0,8},{8,16},{16,24},{1,9},{9,17},{17,25},{2,10},{10,18},{18,26},{... | collective-permute-start | bytes 98312 | tf_op jit(solution)/shard_map/ppermute | solution.py:17
  18.0 3.1 %collective-permute-start.1 = (bf16[32,512]{1,0:T(8,128)(2,1)}, bf16[32,512]{1,0:T(8,128)(2,1)S(1)}, u32[]{:S(2)}, u32[]{:S(2)}) collective-permute-start(bf16[32,512]{1,0:T(8,128)(2,1)} %get-tuple-element.21), channel_id=1, source_target_pairs={{1,0},{2,1},{3,2},{4,3},{5,4},{6,5},{7,6},{0,7},{9,8},{10,9},{11,1... | collective-permute-start | bytes 98312 | tf_op jit(solution)/shard_map/ppermute | solution.py:18
  21.1 0.9 constant_dynamic-update-slice_fusion.4
  22.0 0.7 compare_select_fusion.1
  22.7 0.7 compare_select_fusion
  23.4 2.7 %constant_dynamic-update-slice_fusion.7 = bf16[1536,1536]{1,0:T(8,128)(2,1)} fusion(bf16[1536,512]{1,0:T(8,128)(2,1)} %param.15), kind=kLoop, calls=%fused_computation.96 | loop fusion | bytes 3145728
  26.1 4.8 %gather_fusion.2 = bf16[1536,512]{1,0:T(8,128)(2,1)S(1)} fusion(bf16[512,512]{1,0:T(8,128)(2,1)S(1)} %bitcast.22, s32[2048]{0:T(1024)S(1)} %pad_clamp_fusion), kind=kCustom, calls=%fused_computation.2 | custom fusion | bytes 3151872 | tf_op jit(solution)/shard_map/gather | solution.py:86
  31.0 5.4 %gather_fusion.1 = bf16[1536,512]{1,0:T(8,128)(2,1)} fusion(bf16[256,512]{1,0:T(8,128)(2,1)S(1)} %constant_dynamic-update-slice_fusion, s32[2048]{0:T(1024)S(1)} %pad_clamp_fusion.1), kind=kCustom, calls=%fused_computation.1 | custom fusion | bytes 3151872 | tf_op jit(solution)/shard_map/gather | solution.py:86
  36.5 2.8 %constant_dynamic-update-slice_fusion.6 = bf16[1536,1536]{1,0:T(8,128)(2,1)} fusion(bf16[1536,1536]{1,0:T(8,128)(2,1)} %constant_dynamic-update-slice_fusion.7, bf16[1536,512]{1,0:T(8,128)(2,1)} %gather_fusion.1), kind=kLoop, calls=%fused_computation.95 | loop fusion | bytes 3145728
  39.3 1.3 constant_dynamic-update-slice_fusion.5
  40.6 4.5 %fusion.69 = f32[1536,512]{1,0:T(8,128)S(1)} fusion(bf16[1536,1536]{1,0:T(8,128)(2,1)} %constant_dynamic-update-slice_fusion.5, bf16[1536,512]{1,0:T(8,128)(2,1)S(1)} %copy-done.8), kind=kOutput, calls=%fused_computation.122 | convolution fusion | flops 2415919104 | bytes 9437184 | tf_op jit(solution)/shard_map/dot_general | solution.py:87
  45.1 1.2 fusion.67
  46.3 0.5 copy-done.14
  46.8 0.4 multiply_reduce_fusion.1
  47.2 0.3 copy-done.6
  47.5 1.2 fusion.24
  48.7 0.7 fusion.32
  49.4 0.3 copy-done.9
  49.8 0.5 fusion.68
  50.3 0.5 copy-done.13
  50.8 0.4 copy-done.4
  51.1 0.4 fusion.27
  51.6 1.3 %fusion.63 = (f32[512]{0:T(512)S(1)}, f32[512,512]{1,0:T(8,128)S(1)}, bf16[512,512]{1,0:T(8,128)(2,1)}) fusion(f32[512]{0:T(512)S(1)} %get-tuple-element.23, f32[512,512]{1,0:T(8,128)S(1)} %get-tuple-element.28, f32[512]{0:T(512)S(1)} %broadcast_multiply_fusion.1, f32[512]{0:T(512)S(1)} %get-tuple-element.24, f32[512]{0:T(512)S(1)} %copy-done.5, ...), kind=kLoop, calls=%fused_computation.116 | loop fusion | flops 3407360 | bytes 3680256 | tf_op jit(solution)/shard_map/transpose(jvp())/reduce_sum | solution.py:29
  52.9 3.6 %convolution_convert_fusion.1 = bf16[512,1024]{1,0:T(8,128)(2,1)} fusion(bf16[1024,512]{1,0:T(8,128)(2,1)S(1)} %copy-done, f32[512,512]{1,0:T(8,128)} %copy-done.13, bf16[512,512]{1,0:T(8,128)(2,1)} %param.23, f32[512,512]{1,0:T(8,128)S(1)} %get-tuple-element.7, f32[512]{0:T(512)S(1)} %negate_multiply_fusion.1), kind=kOutput, calls=%fused_computation.40 | convolution fusion | flops 808976384 | bytes 4720640 | tf_op jit(solution)/shard_map/transpose(jvp())/dot_general | solution.py:44
  56.5 3.5 %multiply_reduce_fusion = (f32[1536]{0:T(1024)S(1)}, bf16[1536,512]{0,1:T(8,128)(2,1)S(1)}) fusion(f32[1536,512]{0,1:T(8,128)} %copy-done.2, f32[512]{0:T(512)S(1)} %copy-done.7, f32[1536]{0:T(1024)S(1)} %broadcast_multiply_fusion, bf16[512,1024]{1,0:T(8,128)(2,1)} %convolution_convert_fusion.1, s32[1536]{0:T(1024)S(1)} %copy-done.6), kind=kOutput, calls=%fused_computation.19 | convolution fusion | flops 810809856 | bytes 5263360 | tf_op jit(solution)/shard_map/transpose(jvp())/dot_general | solution.py:42
  60.0 0.9 fusion.45
  61.0 1.0 copy-done.15
  62.1 2.4 %fusion.1 = bf16[1536,512]{1,0:T(8,128)(2,1)S(1)} fusion(f32[1536,512]{1,0:T(8,128)S(1)} %copy-done.15, bf16[512,512]{1,0:T(8,128)(2,1)S(1)} %copy-done.11, f32[1536]{0:T(1024)S(1)} %negate_multiply_fusion, bf16[1536,512]{0,1:T(8,128)(2,1)S(1)} %get-tuple-element.30, f32[1536,512]{0,1:T(8,128)S(1)} %copy-done.3, f32[1536]{0:T(1024)S(1)} %multiply_multiply_fusion, ...), kind=kOutput, calls=%fused_computation.11 | convolution fusion | flops 821035008 | bytes 9988096 | tf_op jit(solution)/shard_map/transpose(jvp())/dot_general | solution.py:36
  64.5 1.2 copy-done.12
  65.7 3.8 %convolution_convert_fusion = bf16[1536,512]{1,0:T(8,128)(2,1)} fusion(bf16[1536,1536]{1,0:T(8,128)(2,1)S(1)} %bitcast.28, bf16[1536,512]{1,0:T(8,128)(2,1)S(1)} %fusion.1), kind=kOutput, calls=%fused_computation.30 | convolution fusion | flops 2416705536 | bytes 7864320 | tf_op jit(solution)/shard_map/dot_general | solution.py:134
  69.5 6.2 %fusion.36 = f32[1536,1024]{1,0:T(8,128)} fusion(bf16[1536,512]{1,0:T(8,128)(2,1)} %copy-done.12, bf16[1536,512]{1,0:T(8,128)(2,1)} %param.19), kind=kOutput, calls=%fused_computation.56 | convolution fusion | flops 1610612736 | bytes 8912896 | tf_op jit(solution)/shard_map/dot_general | solution.py:98
  75.6 10.6 %scatter_custom_fusion.1 = f32[256,512]{1,0:T(8,128)S(1)} fusion(s32[1536]{0:T(1024)} %param.16, f32[1536,1024]{1,0:T(8,128)} %fusion.36, f32[]{:T(128)} %constant.44.clone.1), kind=kCustom, calls=%fused_computation.13 | custom fusion | flops 786432 | bytes 3670528 | tf_op jit(solution)/shard_map/scatter-add | solution.py:104
  86.4 1.3 collective-permute-start.7
  87.7 4.9 %collective-permute-start.6 = (bf16[32,512]{1,0:T(8,128)(2,1)S(1)}, bf16[32,512]{1,0:T(8,128)(2,1)S(1)}, u32[]{:S(2)}, u32[]{:S(2)}) collective-permute-start(bf16[32,512]{1,0:T(8,128)(2,1)S(1)} %get-tuple-element.11), channel_id=1, source_target_pairs={{0,8},{8,16},{16,24},{1,9},{9,17},{17,25},{2,10},{10,18},{18,26},{... | collective-permute-start | bytes 98312 | tf_op jit(solution)/shard_map/ppermute | solution.py:17
  92.6 1.2 convert_add_fusion
  93.8 10.9 %scatter_custom_fusion = f32[512,512]{1,0:T(8,128)S(1)} fusion(f32[512,512]{1,0:T(8,128)S(1)} %convert_add_fusion, s32[1536]{0:T(1024)S(1)} %copy-done.6, f32[1536,1024]{1,0:T(8,128)} %fusion.36), kind=kCustom, calls=%fused_computation.15 | custom fusion | flops 786432 | bytes 4194304 | tf_op jit(solution)/shard_map/scatter-add | solution.py:107
  104.7 0.9 convert_element_type.93
  105.5 3.5 %collective-permute-start.5 = (bf16[32,512]{1,0:T(8,128)(2,1)S(1)}, bf16[32,512]{1,0:T(8,128)(2,1)S(1)}, u32[]{:S(2)}, u32[]{:S(2)}) collective-permute-start(bf16[32,512]{1,0:T(8,128)(2,1)S(1)} %get-tuple-element.12), channel_id=1, source_target_pairs={{1,0},{2,1},{3,2},{4,3},{5,4},{6,5},{7,6},{0,7},{9,8},{10,9},{11,1... | collective-permute-start | bytes 98312 | tf_op jit(solution)/shard_map/ppermute | solution.py:18
  109.1 1.6 %collective-permute-done.4 = bf16[32,512]{1,0:T(8,128)(2,1)S(1)} collective-permute-done((bf16[32,512]{1,0:T(8,128)(2,1)S(1)}, bf16[32,512]{1,0:T(8,128)(2,1)S(1)}, u32[]{:S(2)}, u32[]{:S(2)}) %collective-permute-start.4) | collective-permute-done | bytes 32800 | tf_op jit(solution)/shard_map/ppermute | solution.py:17
  110.7 1.6 %scatter_custom_fusion.2 = f32[128,512]{1,0:T(8,128)S(1)} fusion(f32[128,512]{1,0:T(8,128)S(1)} %slice.96, s32[128]{0:T(128)} %param.18, f32[32,512]{1,0:T(8,128)S(1)} %get-tuple-element.18, f32[]{:T(128)} %constant.50, f32[32,512]{1,0:T(8,128)S(1)} %get-tuple-element.17, f32[32,512]{1,0:T(8,128)S(1)} %get-tuple-element.16, f32[32,512]{1,0:T(8,128)S(1)} %get-tuple-element.15), kind=kCustom, calls=%fused_computation.69 | custom fusion | flops 262144 | bytes 524800 | tf_op jit(solution)/shard_map/scatter-add | solution.py:129
  112.3 0.7 convert_element_type.96
  113.0 13.8 %all-gather = bf16[768,512]{1,0:T(8,128)(2,1)S(1)} all-gather(bf16[192,512]{1,0:T(8,128)(2,1)} %reduce-scatter.2.cloned.1.call-done), channel_id=2, replica_groups=mesh['band'=4,'sector'=8] {'band'}, dimensions={0}, use_global_device_ids=true | all-gather | bytes 983040 | tf_op jit(solution)/shard_map/all_gather | solution.py:141
  126.9 0.8 convert_multiply_fusion.6
  (64 shorter events, 0.7 us)
Async XLA Ops:
  7.2 41.5 %copy-start = (bf16[1024,512]{1,0:T(8,128)(2,1)S(1)}, bf16[1024,512]{1,0:T(8,128)(2,1)}, u32[]{:S(2)}) copy-start(bf16[1024,512]{1,0:T(8,128)(2,1)} %param.22) | copy-start | bytes 3145732
  7.2 18.9 %copy-start.1 = (bf16[8,64,512]{2,1,0:T(8,128)(2,1)S(1)}, bf16[8,64,512]{2,1,0:T(8,128)(2,1)}, u32[]{:S(2)}) copy-start(bf16[8,64,512]{2,1,0:T(8,128)(2,1)} %param.13) | copy-start | bytes 1572868
  7.2 105.8 %reduce-scatter.2.cloned.1.call-start = ((), (), s32[]{:S(2)}) async-start(), calls=%async_computation.1 | async-start | bytes 1769472 | tf_op jit(solution)/shard_map/reduce_scatter | solution.py:133
  11.2 19.8 %collective-permute-start.3 = (bf16[32,512]{1,0:T(8,128)(2,1)}, bf16[32,512]{1,0:T(8,128)(2,1)S(1)}, u32[]{:S(2)}, u32[]{:S(2)}) collective-permute-start(bf16[32,512]{1,0:T(8,128)(2,1)} %get-tuple-element.19), channel_id=1, source_target_pairs={{8,0},{16,8},{24,16},{9,1},{17,9},{25,17},{10,2},{18,10},{26,18},{... | collective-permute-start | bytes 98312 | tf_op jit(solution)/shard_map/ppermute | solution.py:18
  12.5 18.5 %collective-permute-start.2 = (bf16[32,512]{1,0:T(8,128)(2,1)}, bf16[32,512]{1,0:T(8,128)(2,1)S(1)}, u32[]{:S(2)}, u32[]{:S(2)}) collective-permute-start(bf16[32,512]{1,0:T(8,128)(2,1)} %get-tuple-element.20), channel_id=1, source_target_pairs={{0,8},{8,16},{16,24},{1,9},{9,17},{17,25},{2,10},{10,18},{18,26},{... | collective-permute-start | bytes 98312 | tf_op jit(solution)/shard_map/ppermute | solution.py:17
  18.0 12.9 %collective-permute-start.1 = (bf16[32,512]{1,0:T(8,128)(2,1)}, bf16[32,512]{1,0:T(8,128)(2,1)S(1)}, u32[]{:S(2)}, u32[]{:S(2)}) collective-permute-start(bf16[32,512]{1,0:T(8,128)(2,1)} %get-tuple-element.21), channel_id=1, source_target_pairs={{1,0},{2,1},{3,2},{4,3},{5,4},{6,5},{7,6},{0,7},{9,8},{10,9},{11,1... | collective-permute-start | bytes 98312 | tf_op jit(solution)/shard_map/ppermute | solution.py:18
  21.1 9.9 %collective-permute-start = (bf16[32,512]{1,0:T(8,128)(2,1)}, bf16[32,512]{1,0:T(8,128)(2,1)S(1)}, u32[]{:S(2)}, u32[]{:S(2)}) collective-permute-start(bf16[32,512]{1,0:T(8,128)(2,1)} %get-tuple-element.22), channel_id=1, source_target_pairs={{0,1},{1,2},{2,3},{3,4},{4,5},{5,6},{6,7},{7,0},{8,9},{9,10},{10,1... | collective-permute-start | bytes 98312 | tf_op jit(solution)/shard_map/ppermute | solution.py:17
  36.5 4.1 %copy-start.8 = (bf16[1536,512]{1,0:T(8,128)(2,1)S(1)}, bf16[1536,512]{1,0:T(8,128)(2,1)}, u32[]{:S(2)}) copy-start(bf16[1536,512]{1,0:T(8,128)(2,1)} %param.19) | copy-start | bytes 4718596
  40.6 4.5 %copy-start.10 = (bf16[512,512]{1,0:T(8,128)(2,1)S(1)}, bf16[512,512]{1,0:T(8,128)(2,1)}, u32[]{:S(2)}) copy-start(bf16[512,512]{1,0:T(8,128)(2,1)} %param.20) | copy-start | bytes 1572868
  45.1 1.7 %copy-start.14 = (f32[1536,512]{1,0:T(8,128)}, f32[1536,512]{1,0:T(8,128)S(1)}, u32[]{:S(2)}) copy-start(f32[1536,512]{1,0:T(8,128)S(1)} %fusion.69) | copy-start | bytes 9437188
  46.8 1.9 %copy-start.2 = (f32[1536,512]{0,1:T(8,128)}, f32[1536,512]{0,1:T(8,128)S(1)}, u32[]{:S(2)}) copy-start(f32[1536,512]{0,1:T(8,128)S(1)} %get-tuple-element.26) | copy-start | bytes 9437188
  46.8 0.7 copy-start.6
  46.8 0.7 copy-start.7
  48.7 1.0 copy-start.9
  49.7 1.0 copy-start.13
  49.7 1.4 %copy-start.4 = (bf16[8,64,512]{2,1,0:T(8,128)(2,1)S(1)}, bf16[8,64,512]{2,1,0:T(8,128)(2,1)}, u32[]{:S(2)}) copy-start(bf16[8,64,512]{2,1,0:T(8,128)(2,1)} %param.25) | copy-start | bytes 1572868
  49.8 1.4 %copy-start.5 = (f32[512]{0:T(512)S(1)}, f32[512]{0:T(512)}, u32[]{:S(2)}) copy-start(f32[512]{0:T(512)} %param.24) | copy-start | bytes 6148
  56.5 3.5 %copy-start.3 = (f32[1536,512]{0,1:T(8,128)S(1)}, f32[1536,512]{0,1:T(8,128)}, u32[]{:S(2)}) copy-start(f32[1536,512]{0,1:T(8,128)} %copy-done.2) | copy-start | bytes 9437188
  60.0 1.0 copy-start.11
  60.0 2.1 %copy-start.15 = (f32[1536,512]{1,0:T(8,128)S(1)}, f32[1536,512]{1,0:T(8,128)}, u32[]{:S(2)}) copy-start(f32[1536,512]{1,0:T(8,128)} %copy-done.14) | copy-start | bytes 9437188
  60.0 5.7 %slice-start = ((s8[4718592]{0:T(1024)(128)(4,1)}), s8[4194304]{0:T(1024)(128)(4,1)S(1)}, s32[]{:S(2)}) async-start(s8[4718592]{0:T(1024)(128)(4,1)} %bitcast.27), calls=%async_computation.2 | async-start | bytes 8388608
  62.1 3.6 %slice-start.1 = ((s8[4718592]{0:T(1024)(128)(4,1)}), s8[524288]{0:T(1024)(128)(4,1)S(1)}, s32[]{:S(2)}) async-start(s8[4718592]{0:T(1024)(128)(4,1)} %bitcast.27), calls=%async_computation.3 | async-start | bytes 1048576
  64.5 1.2 copy-start.12
  86.4 22.7 %collective-permute-start.7 = (bf16[32,512]{1,0:T(8,128)(2,1)S(1)}, bf16[32,512]{1,0:T(8,128)(2,1)S(1)}, u32[]{:S(2)}, u32[]{:S(2)}) collective-permute-start(bf16[32,512]{1,0:T(8,128)(2,1)S(1)} %get-tuple-element.10), channel_id=1, source_target_pairs={{8,0},{16,8},{24,16},{9,1},{17,9},{25,17},{10,2},{18,10},{26,18},{... | collective-permute-start | bytes 98312 | tf_op jit(solution)/shard_map/ppermute | solution.py:18
  87.7 21.4 %collective-permute-start.6 = (bf16[32,512]{1,0:T(8,128)(2,1)S(1)}, bf16[32,512]{1,0:T(8,128)(2,1)S(1)}, u32[]{:S(2)}, u32[]{:S(2)}) collective-permute-start(bf16[32,512]{1,0:T(8,128)(2,1)S(1)} %get-tuple-element.11), channel_id=1, source_target_pairs={{0,8},{8,16},{16,24},{1,9},{9,17},{17,25},{2,10},{10,18},{18,26},{... | collective-permute-start | bytes 98312 | tf_op jit(solution)/shard_map/ppermute | solution.py:17
  105.5 5.1 %collective-permute-start.4 = (bf16[32,512]{1,0:T(8,128)(2,1)S(1)}, bf16[32,512]{1,0:T(8,128)(2,1)S(1)}, u32[]{:S(2)}, u32[]{:S(2)}) collective-permute-start(bf16[32,512]{1,0:T(8,128)(2,1)S(1)} %get-tuple-element.9), channel_id=1, source_target_pairs={{0,1},{1,2},{2,3},{3,4},{4,5},{5,6},{6,7},{7,0},{8,9},{9,10},{10,1... | collective-permute-start | bytes 98312 | tf_op jit(solution)/shard_map/ppermute | solution.py:17
  105.5 5.1 %collective-permute-start.5 = (bf16[32,512]{1,0:T(8,128)(2,1)S(1)}, bf16[32,512]{1,0:T(8,128)(2,1)S(1)}, u32[]{:S(2)}, u32[]{:S(2)}) collective-permute-start(bf16[32,512]{1,0:T(8,128)(2,1)S(1)} %get-tuple-element.12), channel_id=1, source_target_pairs={{1,0},{2,1},{3,2},{4,3},{5,4},{6,5},{7,6},{0,7},{9,8},{10,9},{11,1... | collective-permute-start | bytes 98312 | tf_op jit(solution)/shard_map/ppermute | solution.py:18
Sparse Core Ops, SparseCore 0:
  69.6 35.3 reduce-scatter.1
